TPU v7x, 256 devices: a whole 4x4x8 slice. The times are simulated.
256 devices in a mesh: rep: 32 (over x, y, core), tp: 8 (over z).
Axes of the slice: x: 4, y: 4, z: 8, core: 2. Of those that a mesh axis runs over, the one named last changes fastest.
Arguments:
- hidden_in: bfloat16 [3072, 8192], P('rep', 'tp'), may hold values from -6 to 6
- queries: bfloat16 [3072, 8192], P('rep', 'tp'), may hold values from -20 to 20
- cache_keys: bfloat16 [3072, 128, 1024], P('rep', None, 'tp'), may hold values from -6 to 6
- cached_value_rows: bfloat16 [3072, 128, 1024], P('rep', None, 'tp'), may hold values from -6 to 6
- cache_lengths: int32 [3072], P('rep'), may hold values from 1 to 128, 98304 in all
- base_key_matrix: bfloat16 [8192, 1024], P(None, 'tp'), may hold values from -0.0625 to 0.0625
- base_value_matrix: bfloat16 [8192, 1024], P(None, 'tp'), may hold values from -0.0625 to 0.0625
- shrink_weights: bfloat16 [128, 8192, 128], P('rep', 'tp'), may hold values from -0.0625 to 0.0625
- pooled_up_weights: bfloat16 [128, 2, 64, 1024], P('rep', None, None, 'tp'), may hold values from -0.75 to 0.75
- block_owner: int32 [768, 1], P('rep'), may hold values from 0 to 31; in each aligned block of 24 rows (0 to 23, 24 to 47, ...) at most 2 rows name the same one
- block_slot: int32 [768], P('rep'), may hold values from 0 to 3
Outputs:
- new_keys: bfloat16 [3072, 1024], P('rep', 'tp')
- new_values: bfloat16 [3072, 1024], P('rep', 'tp')
- context: bfloat16 [3072, 8192], P('rep', 'tp')
Inputs may be any that keep to these rules, and one draw needn't show every extreme that they name: `block_owner`: among the 24 blocks of one replica group at most 2 name the same owner, and some group in every draw has 2 blocks with one owner.
All inputs are finite; a program needn't handle non-finite values. No bound on the sum of `cache_lengths` on one device may be relied on, other than what follows from the above.
Results may differ from a plain program's by a relative error of at most 0.0055.
Values may be sent and summed in bfloat16 or wider, within the bound.
A program may use at most 128 MiB of HBM per device.

v0:
```python
import jax
import jax.numpy as jnp
from jax import lax
from jax.sharding import PartitionSpec as P

HEAD_SIZE = 128
BLK = 4
adapter_scale = 0.5
masked_score = -1e30


def attend(group_queries, key_cache, value_cache, lengths, fresh_keys, fresh_values):
    rows_here = group_queries.shape[0]
    head_groups = key_cache.shape[2] // HEAD_SIZE
    group_size = group_queries.shape[1] // (head_groups * HEAD_SIZE)
    window = key_cache.shape[1]
    inverse_root = HEAD_SIZE ** (-0.5)
    query_heads = group_queries.reshape(rows_here, head_groups, group_size, HEAD_SIZE)
    key_heads = key_cache.reshape(rows_here, window, head_groups, HEAD_SIZE)
    value_heads = value_cache.reshape(rows_here, window, head_groups, HEAD_SIZE)
    scores = (
        jnp.einsum("rkgd,rtkd->rkgt", query_heads, key_heads, preferred_element_type=jnp.float32)
        * inverse_root
    )
    own_score = (
        jnp.einsum(
            "rkgd,rkd->rkg",
            query_heads,
            fresh_keys.reshape(rows_here, head_groups, HEAD_SIZE),
            preferred_element_type=jnp.float32,
        )
        * inverse_root
    )
    visible = (jnp.arange(window, dtype=jnp.int32)[None, :] < lengths[:, None])[:, None, None, :]
    highest = jnp.maximum(jnp.max(jnp.where(visible, scores, masked_score), axis=-1), own_score)
    exp_terms = jnp.where(visible, jnp.exp(scores - highest[..., None]), 0.0)
    own_term = jnp.exp(own_score - highest)
    denominator = jnp.sum(exp_terms, axis=-1) + own_term
    weights = (exp_terms / denominator[..., None]).astype(jnp.bfloat16)
    own_weight = (own_term / denominator).astype(jnp.bfloat16)
    context = jnp.einsum(
        "rkgt,rtkd->rkgd", weights, value_heads, preferred_element_type=jnp.float32
    )
    context = context + own_weight.astype(jnp.float32)[..., None] * fresh_values.reshape(
        rows_here, head_groups, 1, HEAD_SIZE
    ).astype(jnp.float32)
    return context.reshape(rows_here, -1).astype(jnp.bfloat16)


def earlier_ranks(owners):
    span_count = owners.shape[-1]
    matching = owners[..., :, None] == owners[..., None, :]
    before = jnp.arange(span_count)[:, None] > jnp.arange(span_count)[None, :]
    return jnp.sum((matching & before).astype(jnp.int32), axis=-1)


def slot_layout(owners_all, slots_all, myself, replicas, blocks_here, capacity):
    owners_grid = owners_all.reshape(replicas, blocks_here)
    slots_grid = slots_all.reshape(replicas, blocks_here)
    ranks_grid = earlier_ranks(owners_grid)
    placed = (owners_grid == myself)[:, :, None] & (
        ranks_grid[:, :, None] == jnp.arange(capacity, dtype=jnp.int32)[None, None, :]
    )
    placed_int = placed.astype(jnp.int32)
    slot_index = jnp.sum(placed_int * slots_grid[:, :, None], axis=1).reshape(replicas * capacity)
    return (placed, slot_index)


def adapter_pass(slot_rows, slot_index, shrink_weights, pooled_up_weights, site_sum):
    chosen_shrink = jnp.take(shrink_weights, slot_index, axis=0)
    selected_expand = jnp.take(pooled_up_weights, slot_index, axis=0)
    partial_value = jnp.einsum(
        "snd,sdr->snr", slot_rows, chosen_shrink, preferred_element_type=jnp.float32
    )
    shrunk = site_sum(partial_value).astype(jnp.bfloat16)
    split_halves = shrunk.reshape(shrunk.shape[0], shrunk.shape[1], 2, shrunk.shape[2] // 2)
    summed_terms = jnp.einsum(
        "snkr,skrw->snkw", split_halves, selected_expand, preferred_element_type=jnp.float32
    )
    return (adapter_scale * summed_terms).astype(jnp.bfloat16)


def shards(
    hidden_in,
    queries,
    cache_keys,
    cached_value_rows,
    cache_lengths,
    base_key_matrix,
    base_value_matrix,
    shrink_weights,
    pooled_up_weights,
    block_owner,
    block_slot,
):
    rows_here = hidden_in.shape[0]
    shard_width = hidden_in.shape[1]
    replicas = lax.axis_size("rep")
    myself = lax.axis_index("rep")
    blocks_here = rows_here // BLK
    capacity = max(2, (2 * blocks_here + replicas - 1) // replicas)
    key_row_width = base_key_matrix.shape[1]
    gathered = lax.all_gather(hidden_in, "tp", axis=1, tiled=True)
    base_keys = jnp.dot(gathered, base_key_matrix, preferred_element_type=jnp.float32)
    base_values = jnp.dot(gathered, base_value_matrix, preferred_element_type=jnp.float32)
    owners_all, slots_all = (
        lax.all_gather(block_owner[:, 0], "rep", axis=0, tiled=True),
        lax.all_gather(block_slot, "rep", axis=0, tiled=True),
    )
    placed, slot_index = slot_layout(owners_all, slots_all, myself, replicas, blocks_here, capacity)
    every_row = lax.all_gather(hidden_in, "rep", axis=0, tiled=True)
    same_group = jnp.eye(replicas, dtype=jnp.bfloat16)
    compactor = jnp.einsum("pq,qbc->pcqb", same_group, placed.astype(jnp.bfloat16)).reshape(
        replicas * capacity, replicas * blocks_here
    )
    slot_rows = jnp.dot(
        compactor,
        every_row.reshape(replicas * blocks_here, BLK * shard_width),
        preferred_element_type=jnp.float32,
    ).astype(jnp.bfloat16)
    slot_rows = slot_rows.reshape(replicas * capacity, BLK, shard_width)

    def sum_every(partial_value):
        return lax.psum(partial_value, "tp")

    deltas = adapter_pass(slot_rows, slot_index, shrink_weights, pooled_up_weights, sum_every)
    spread = jnp.einsum(
        "sq,sx->qx",
        compactor,
        deltas.reshape(replicas * capacity, BLK * 2 * key_row_width),
        preferred_element_type=jnp.float32,
    )
    spread = spread.reshape(replicas * rows_here, 2, key_row_width)
    per_row_delta = lax.psum_scatter(
        spread.astype(jnp.bfloat16), "rep", scatter_dimension=0, tiled=True
    ).astype(jnp.float32)
    fresh_keys = (base_keys + per_row_delta[:, 0]).astype(jnp.bfloat16)
    fresh_values = (base_values + per_row_delta[:, 1]).astype(jnp.bfloat16)
    context = attend(
        queries, cache_keys, cached_value_rows, cache_lengths, fresh_keys, fresh_values
    )
    return (fresh_keys, fresh_values, context)


def solution(mesh):
    return jax.shard_map(
        shards,
        mesh=mesh,
        in_specs=(
            P("rep", "tp"),
            P("rep", "tp"),
            P("rep", None, "tp"),
            P("rep", None, "tp"),
            P("rep"),
            P(None, "tp"),
            P(None, "tp"),
            P("rep", "tp", None),
            P("rep", None, None, "tp"),
            P("rep", None),
            P("rep"),
        ),
        out_specs=(P("rep", "tp"), P("rep", "tp"), P("rep", "tp")),
        check_vma=False,
    )
```

profile of v0, /device:TPU:2, one launch (start us, length us, event | category | flops | bytes accessed | tf_op | source)
XLA Modules:
  0.0 236.1 jit_solution(2521708871560459143)
XLA Ops:
  8.0 0.0 all-gather.6.cloned.1.call-start
  8.1 0.7 all-gather.6.cloned.1.call-update
  8.8 0.0 reduce-scatter.2.cloned.1.call-start
  8.8 1.4 dynamic-slice
  10.9 0.9 dynamic-update-slice.1
  11.8 0.7 bitcast_dynamic-update-slice_fusion
  12.5 15.9 %all-reduce.2 = (s32[768]{0:T(1024)S(1)}, s32[768]{0:T(1024)S(1)}) all-reduce(s32[768]{0:T(1024)S(1)} %bitcast_dynamic-update-slice_fusion, s32[768]{0:T(1024)S(1)} %dynamic-update-slice.1), channel_id=2, replica_groups=mesh['rep'=32,'tp'=8] {'rep'}, use_global_device_ids=true, to_apply=%add | all-reduce | flops 1536 | bytes 12288
  28.4 0.1 reshape.169
  28.5 0.1 copy.23
  28.5 0.2 convert_reduce_fusion
  28.7 0.1 copy.25
  28.8 0.1 mul.45
  28.9 0.1 select_reduce_fusion.1
  29.0 0.1 copy.26
  29.1 0.1 reshape.172
  29.2 0.1 reshape.171
  29.3 1.0 multiply_bitcast_fusion
  30.3 1.7 reshape.170
  32.1 2.1 gather_fusion
  34.2 8.6 %gather_fusion.1 = bf16[64,1024,128]{2,1,0:T(8,128)(2,1)} fusion(bf16[4,1024,128]{2,1,0:T(8,128)(2,1)} %param.18, s32[1024]{0:T(1024)S(1)} %pad_clamp_fusion), kind=kCustom, calls=%fused_computation.1 | custom fusion | bytes 33554688 | tf_op jit(solution)/shard_map/jit(_take)/gather | solution.py:70
  42.8 24.6 %all-gather.6.cloned.1.call-done = bf16[3072,1024]{1,0:T(8,128)(2,1)} async-done(((bf16[96,1024]{1,0:T(8,128)(2,1)}), bf16[3072,1024]{1,0:T(8,128)(2,1)}) %all-gather.6.cloned.1.call-update) | async-done | bytes 6291472 | tf_op jit(solution)/shard_map/all_gather | solution.py:111
  67.4 10.7 %reshape.173 = bf16[768,4096]{1,0:T(8,128)(2,1)} reshape(bf16[3072,1024]{1,0:T(8,128)(2,1)} %all-gather.6.cloned.1.call-done) | data formatting | bytes 12582912 | tf_op jit(solution)/shard_map/reshape | solution.py:118
  78.1 4.8 %convolution_convert_fusion = bf16[64,4096]{1,0:T(8,128)(2,1)} fusion(bf16[64,768]{1,0:T(8,128)(2,1)S(1)} %reshape.170, bf16[768,4096]{1,0:T(8,128)(2,1)} %reshape.173), kind=kOutput, calls=%fused_computation.6 | convolution fusion | flops 402915328 | bytes 6914048 | tf_op jit(solution)/shard_map/dot_general | solution.py:116
  82.9 2.2 reshape.174
  85.1 8.7 %fusion = f32[64,4,128]{2,1,0:T(4,128)S(1)} fusion(bf16[64,4,1024]{2,1,0:T(4,128)(2,1)} %reshape.174, bf16[64,1024,128]{2,1,0:T(8,128)(2,1)} %gather_fusion.1, pred[64]{0:T(512)(128)(4,1)S(1)} %compare_and_fusion), kind=kOutput, calls=%fused_computation.2 | convolution fusion | flops 75497472 | bytes 17432640 | tf_op jit(solution)/shard_map/snd,sdr->snr/dot_general | solution.py:72
  93.7 31.5 %all-reduce.4 = bf16[64,4,128]{2,1,0:T(4,128)(2,1)S(1)} all-reduce(f32[64,4,128]{2,1,0:T(4,128)S(1)} %fusion), channel_id=1, replica_groups=mesh['rep'=32,'tp'=8] {'tp'}, use_global_device_ids=true, to_apply=%region_2.3 | all-reduce | flops 32768 | bytes 196608 | tf_op jit(solution)/shard_map/psum | solution.py:124
  125.2 0.1 reshape.175
  125.3 2.3 fusion.14
  127.6 0.1 copy.29
  127.8 0.1 reshape.176
  127.8 1.7 convolution_convert_fusion.1
  129.6 3.8 %convert_element_type.61 = bf16[3072,2,128]{2,1,0:T(2,128)(2,1)} reshape(bf16[768,1024]{1,0:T(8,128)(2,1)} %convolution_convert_fusion.1) | data formatting | bytes 3145728 | tf_op jit(solution)/shard_map/convert_element_type | solution.py:135
  133.4 2.8 %copy.30 = bf16[3072,2,128]{2,0,1:T(8,128)(2,1)} copy(bf16[3072,2,128]{2,1,0:T(2,128)(2,1)} %convert_element_type.61) | data formatting | bytes 3145728 | tf_op jit(solution)/shard_map/convert_element_type | solution.py:135
  136.2 0.0 reduce-scatter.2.cloned.1.call-update
  136.2 0.2 all-gather.4.cloned.1.call-start
  136.5 0.3 all-gather.4.cloned.1.call-update
  136.9 0.1 iota_compare_fusion
  137.0 0.6 copy-done.4
  137.5 2.4 %select_reduce_fusion = (f32[96,8]{1,0:T(8,128)}, f32[96,8,128]{2,1,0:T(8,128)S(1)}) fusion(pred[96,128]{1,0:T(8,128)(4,1)S(1)} %iota_compare_fusion, bf16[96,8,128]{2,1,0:T(8,128)(2,1)S(1)} %bitcast.43, bf16[96,128,128]{2,1,0:T(8,128)(2,1)S(1)} %copy-done), kind=kOutput, calls=%fused_computation.25 | convolution fusion | flops 25459968 | bytes 3750912 | tf_op jit(solution)/shard_map/rkgd,rtkd->rkgt/dot_general | solution.py:22
  140.0 79.3 %reduce-scatter.2.cloned.1.call-done = bf16[96,2,128]{2,0,1:T(8,128)(2,1)} async-done(((bf16[3072,2,128]{2,0,1:T(8,128)(2,1)}), bf16[96,2,128]{2,0,1:T(8,128)(2,1)}) %reduce-scatter.2.cloned.1.call-update) | async-done | bytes 49168 | tf_op jit(solution)/shard_map/reduce_scatter | solution.py:134
  219.3 1.4 convert_element_type.62
  220.8 2.8 %fusion.17 = bf16[96,128]{1,0:T(8,128)(2,1)S(1)} fusion(bf16[96,8192]{1,0:T(8,128)(2,1)} %all-gather.4.cloned.1.call-done, bf16[8192,128]{1,0:T(8,128)(2,1)} %param.16, f32[96,2,128]{2,0,1:T(8,128)} %convert_element_type.62), kind=kOutput, calls=%fused_computation.19 | convolution fusion | flops 201351168 | bytes 3743744 | tf_op jit(solution)/shard_map/dot_general | solution.py:104
  223.6 1.2 fusion.26
  224.8 0.3 fusion.20
  225.1 1.2 fusion.38
  226.3 0.6 copy-done.10
  227.0 1.0 fusion.7
  228.0 0.7 copy.40
  (33 shorter events, 0.2 us)
Async XLA Ops:
  8.0 129.6 %copy-start = (bf16[96,128,128]{2,1,0:T(8,128)(2,1)S(1)}, bf16[96,128,128]{2,1,0:T(8,128)(2,1)}, u32[]{:S(2)}) copy-start(bf16[96,128,128]{2,1,0:T(8,128)(2,1)} %param.13) | copy-start | bytes 9437188
  8.0 24.0 %copy-start.1 = (bf16[4,2,64,128]{3,2,1,0:T(8,128)(2,1)S(1)}, bf16[4,2,64,128]{3,2,1,0:T(8,128)(2,1)}, u32[]{:S(2)}) copy-start(bf16[4,2,64,128]{3,2,1,0:T(8,128)(2,1)} %param.19) | copy-start | bytes 393220
  8.0 59.3 %all-gather.6.cloned.1.call-start = ((), (), s32[]{:S(2)}) async-start(), calls=%async_computation.2 | async-start | bytes 6488064 | tf_op jit(solution)/shard_map/all_gather | solution.py:111
  8.8 210.6 %reduce-scatter.2.cloned.1.call-start = ((), (), s32[]{:S(2)}) async-start(), calls=%async_computation.3 | async-start | bytes 1622016 | tf_op jit(solution)/shard_map/reduce_scatter | solution.py:134
  133.4 3.4 %copy-start.7 = (bf16[96,1024]{1,0:T(8,128)(2,1)S(1)}, bf16[96,1024]{1,0:T(8,128)(2,1)}, u32[]{:S(2)}) copy-start(bf16[96,1024]{1,0:T(8,128)(2,1)} %param.12) | copy-start | bytes 589828
  133.4 3.5 %copy-start.9 = (s32[96]{0:T(128)S(1)}, s32[96]{0:T(128)}, u32[]{:S(2)}) copy-start(s32[96]{0:T(128)} %param.15) | copy-start | bytes 1156
  136.2 84.5 %all-gather.4.cloned.1.call-start = ((), (), s32[]{:S(2)}) async-start(), calls=%async_computation.1 | async-start | bytes 1769472 | tf_op jit(solution)/shard_map/all_gather | solution.py:103
  136.9 0.7 copy-start.4
  220.8 4.0 %copy-start.5 = (f32[96,8]{1,0:T(8,128)S(1)}, f32[96,8]{1,0:T(8,128)}, u32[]{:S(2)}) copy-start(f32[96,8]{1,0:T(8,128)} %get-tuple-element.9) | copy-start | bytes 9220
  220.8 4.4 %copy-start.2 = (bf16[96,8192]{1,0:T(8,128)(2,1)S(1)}, bf16[96,8192]{1,0:T(8,128)(2,1)}, u32[]{:S(2)}) copy-start(bf16[96,8192]{1,0:T(8,128)(2,1)} %all-gather.4.cloned.1.call-done) | copy-start | bytes 4718596
  220.8 4.4 %copy-start.3 = (bf16[8192,128]{1,0:T(8,128)(2,1)S(1)}, bf16[8192,128]{1,0:T(8,128)(2,1)}, u32[]{:S(2)}) copy-start(bf16[8192,128]{1,0:T(8,128)(2,1)} %param.17) | copy-start | bytes 6291460
  220.8 4.4 %copy-start.6 = (f32[96,2,128]{2,0,1:T(8,128)S(1)}, f32[96,2,128]{2,0,1:T(8,128)}, u32[]{:S(2)}) copy-start(f32[96,2,128]{2,0,1:T(8,128)} %convert_element_type.62) | copy-start | bytes 294916
  223.5 2.8 %copy-start.8 = (bf16[96,128]{1,0:T(8,128)(2,1)}, bf16[96,128]{1,0:T(8,128)(2,1)S(1)}, u32[]{:S(2)}) copy-start(bf16[96,128]{1,0:T(8,128)(2,1)S(1)} %fusion.17) | copy-start | bytes 73732
  225.1 1.9 copy-start.10
Sparse Core Ops, SparseCore 0:
  11.4 55.9 all-gather.5
  136.3 82.9 reduce-scatter.1
Sparse Core Ops, SparseCore 1:
  138.5 36.9 all-gather.3
where the time goes:
time: 237 us; the launch traced here: 236 us
  waiting for transfers between devices  105 us (44%)
  blocking collectives  47.3 us (20%)
  local copies, waits for them, and re-layouts  37.9 us (16%)
  matrix products  26 us (11%)
  between operations  16.4 us (7%)
  other arithmetic  3.18 us (1%)
    reduce_scatter x1, waiting for transfers between devices, shards(): lax.psum_scatter(spread.astype(jnp.bfloat16), 'rep', scatter_dimension=0,...  79.3 us
    psum x1, blocking collectives, sum_every(): return lax.psum(partial_value, 'tp')  31.5 us
    all_gather x1, waiting for transfers between devices, shards(): every_row = lax.all_gather(hidden_in, 'rep', axis=0, tiled=True)  24.6 us
    unnamed x1, blocking collectives  15.9 us
    reshape x1, local copies, waits for them, and re-layouts, shards(): every_row.reshape(replicas * blocks_here, BLK * shard_width)  10.7 us
    dot_general x1, matrix products, adapter_pass(): jnp.einsum('snd,sdr->snr', slot_rows, chosen_shrink, preferred_element_ty...  8.66 us
    gather x1, local copies, waits for them, and re-layouts, adapter_pass(): chosen_shrink = jnp.take(shrink_weights, slot_index, axis=0)  8.6 us
    convert_element_type x2, local copies, waits for them, and re-layouts, shards(): spread.astype(jnp.bfloat16)  6.61 us
  transfers between devices with their start and end apart: 3, of which 2 were waited for; matrix products, arithmetic and copies ran while one was open for 9% of the time, Pallas kernels for 0%

commit v1 on v0

--- a/solution.py
+++ b/solution.py
@@ -108,7 +108,10 @@
         lax.all_gather(block_slot, "rep", axis=0, tiled=True),
     )
     placed, slot_index = slot_layout(owners_all, slots_all, myself, replicas, blocks_here, capacity)
-    every_row = lax.all_gather(hidden_in, "rep", axis=0, tiled=True)
+    devices = lax.axis_size("rep")
+    blocks = jnp.stack([hidden_in for _ in range(devices)])
+    blocks = lax.all_to_all(blocks, "rep", split_axis=0, concat_axis=0)
+    every_row = jnp.concatenate(blocks, axis=0)
     same_group = jnp.eye(replicas, dtype=jnp.bfloat16)
     compactor = jnp.einsum("pq,qbc->pcqb", same_group, placed.astype(jnp.bfloat16)).reshape(
         replicas * capacity, replicas * blocks_here

time: 237 us -> 295 us (1.24)
  blocking collectives: 47.3 us -> 114 us
  waiting for transfers between devices: 105 us -> 86 us
  starting transfers between devices: 0.3 us -> 8.07 us
    unnamed x1, blocking collectives: 15.9 us -> 79.9 us
    all_gather x1 -> x0, waiting for transfers between devices: 24.6 us -> none  [shards(): every_row = lax.all_gather(hidden_in, 'rep', axis=0, tiled=True)]
    another operation x0 -> x2, local copies, waits for them, and re-layouts: none -> 15.3 us  [the longest x1 10.7 us: shards(): every_row.reshape(replicas * blocks_here, BLK * shard_width)]
    reshape x1 -> x0, local copies, waits for them, and re-layouts: 10.7 us -> none  [shards(): every_row.reshape(replicas * blocks_here, BLK * shard_width)]
    all_to_all x0 -> x1, starting transfers between devices: none -> 7.81 us  [shards(): blocks = lax.all_to_all(blocks, 'rep', split_axis=0, concat_axis=0)]
    reduce_scatter x1, waiting for transfers between devices: 79.3 us -> 85.6 us  [shards(): lax.psum_scatter(spread.astype(jnp.bfloat16), 'rep', scatter_dimension=0,...]
  transfers between devices with their start and end apart: 3 -> 3, of which waited for: 2 -> 1; matrix products, arithmetic and copies ran while one was open for 9% -> 7% of each run, Pallas kernels for 0% -> 0%
where the time goes in v1:
time: 295 us; the launch traced here: 294 us
  blocking collectives  114 us (39%)
  waiting for transfers between devices  86 us (29%)
  local copies, waits for them, and re-layouts  40.3 us (14%)
  matrix products  26.1 us (9%)
  between operations  16.4 us (6%)
  starting transfers between devices  8.07 us (3%)
  other arithmetic  3.17 us (1%)
    reduce_scatter x1, waiting for transfers between devices, shards(): lax.psum_scatter(spread.astype(jnp.bfloat16), 'rep', scatter_dimension=0,...  85.6 us
    unnamed x1, blocking collectives  79.9 us
    psum x1, blocking collectives, sum_every(): return lax.psum(partial_value, 'tp')  34 us
    another operation x1, local copies, waits for them, and re-layouts, shards(): every_row.reshape(replicas * blocks_here, BLK * shard_width)  10.7 us
    dot_general x1, matrix products, adapter_pass(): jnp.einsum('snd,sdr->snr', slot_rows, chosen_shrink, preferred_element_ty...  8.66 us
    gather x1, local copies, waits for them, and re-layouts, adapter_pass(): chosen_shrink = jnp.take(shrink_weights, slot_index, axis=0)  8.59 us
    all_to_all x1, starting transfers between devices, shards(): blocks = lax.all_to_all(blocks, 'rep', split_axis=0, concat_axis=0)  7.81 us
    convert_element_type x2, local copies, waits for them, and re-layouts, shards(): spread.astype(jnp.bfloat16)  6.6 us
  transfers between devices with their start and end apart: 3, of which 1 were waited for; matrix products, arithmetic and copies ran while one was open for 7% of the time, Pallas kernels for 0%

profile of v1, /device:TPU:2, one launch (start us, length us, event | category | flops | bytes accessed | tf_op | source)
XLA Modules:
  0.0 294.0 jit_solution(8083053023596823827)
XLA Ops:
  8.0 0.0 copy-start
  8.0 4.5 %stack.2 = bf16[32,96,1024]{2,1,0:T(8,128)(2,1)} broadcast(bf16[96,1024]{1,0:T(8,128)(2,1)} %param.11), dimensions={1,2} | broadcast | bytes 6488064 | tf_op jit(solution)/shard_map/stack | solution.py:112
  12.5 7.8 %all-to-all-start = ((bf16[32,96,1024]{2,1,0:T(8,128)(2,1)}), bf16[32,96,1024]{2,1,0:T(8,128)(2,1)}, u32[]{:S(2)}, u32[]{:S(2)}) async-start(bf16[32,96,1024]{2,1,0:T(8,128)(2,1)} %stack.2), calls=%async_computation | async-start | bytes 12582912 | tf_op jit(solution)/shard_map/all_to_all | solution.py:113
  20.4 0.0 reduce-scatter.2.cloned.1.call-start
  20.4 0.6 dynamic-slice
  21.7 0.2 dynamic-update-slice.1
  21.9 0.1 bitcast_dynamic-update-slice_fusion
  22.0 79.9 %all-reduce.2 = (s32[768]{0:T(1024)S(1)}, s32[768]{0:T(1024)S(1)}) all-reduce(s32[768]{0:T(1024)S(1)} %bitcast_dynamic-update-slice_fusion, s32[768]{0:T(1024)S(1)} %dynamic-update-slice.1), channel_id=2, replica_groups=mesh['rep'=32,'tp'=8] {'rep'}, use_global_device_ids=true, to_apply=%add | all-reduce | flops 1536 | bytes 12288
  101.9 0.1 reshape.168
  102.0 0.1 copy.23
  102.1 0.2 convert_reduce_fusion
  102.3 0.1 copy.25
  102.3 0.1 mul.45
  102.5 0.1 select_reduce_fusion.1
  102.6 0.1 copy.26
  102.7 0.1 reshape.171
  102.8 0.1 reshape.170
  102.9 1.0 multiply_bitcast_fusion
  103.9 1.7 reshape.169
  105.6 2.2 gather_fusion
  107.8 8.6 %gather_fusion.1 = bf16[64,1024,128]{2,1,0:T(8,128)(2,1)} fusion(bf16[4,1024,128]{2,1,0:T(8,128)(2,1)} %param.18, s32[1024]{0:T(1024)S(1)} %pad_clamp_fusion), kind=kCustom, calls=%fused_computation.1 | custom fusion | bytes 33554688 | tf_op jit(solution)/shard_map/jit(_take)/gather | solution.py:70
  116.4 10.7 %reshape_reshape.3 = bf16[768,4096]{1,0:T(8,128)(2,1)} reshape(bf16[32,96,1024]{2,1,0:T(8,128)(2,1)} %all-to-all-done) | data formatting | bytes 12582912 | tf_op jit(solution)/shard_map/reshape;reshape | solution.py:121
  127.1 4.8 %convolution_convert_fusion = bf16[64,4096]{1,0:T(8,128)(2,1)} fusion(bf16[64,768]{1,0:T(8,128)(2,1)S(1)} %reshape.169, bf16[768,4096]{1,0:T(8,128)(2,1)} %reshape_reshape.3), kind=kOutput, calls=%fused_computation.6 | convolution fusion | flops 402915328 | bytes 6914048 | tf_op jit(solution)/shard_map/dot_general | solution.py:119
  131.9 2.2 reshape.172
  134.1 8.7 %fusion = f32[64,4,128]{2,1,0:T(4,128)S(1)} fusion(bf16[64,4,1024]{2,1,0:T(4,128)(2,1)} %reshape.172, bf16[64,1024,128]{2,1,0:T(8,128)(2,1)} %gather_fusion.1, pred[64]{0:T(512)(128)(4,1)S(1)} %compare_and_fusion), kind=kOutput, calls=%fused_computation.2 | convolution fusion | flops 75497472 | bytes 17432640 | tf_op jit(solution)/shard_map/snd,sdr->snr/dot_general | solution.py:72
  142.8 34.0 %all-reduce.4 = bf16[64,4,128]{2,1,0:T(4,128)(2,1)S(1)} all-reduce(f32[64,4,128]{2,1,0:T(4,128)S(1)} %fusion), channel_id=1, replica_groups=mesh['rep'=32,'tp'=8] {'tp'}, use_global_device_ids=true, to_apply=%region_2.3 | all-reduce | flops 32768 | bytes 196608 | tf_op jit(solution)/shard_map/psum | solution.py:127
  176.8 0.1 reshape.173
  176.9 2.3 fusion.14
  179.2 0.1 copy.29
  179.3 0.1 reshape.174
  179.4 1.7 convolution_convert_fusion.1
  181.2 3.8 %convert_element_type.61 = bf16[3072,2,128]{2,1,0:T(2,128)(2,1)} reshape(bf16[768,1024]{1,0:T(8,128)(2,1)} %convolution_convert_fusion.1) | data formatting | bytes 3145728 | tf_op jit(solution)/shard_map/convert_element_type | solution.py:138
  185.0 2.8 copy.30
  187.8 0.0 reduce-scatter.2.cloned.1.call-update
  187.8 0.2 all-gather.3.cloned.1.call-start
  188.0 0.3 all-gather.3.cloned.1.call-update
  188.4 0.1 iota_compare_fusion
  188.5 0.6 copy-done.4
  189.1 2.4 select_reduce_fusion
  191.5 85.6 %reduce-scatter.2.cloned.1.call-done = bf16[96,2,128]{2,0,1:T(8,128)(2,1)} async-done(((bf16[3072,2,128]{2,0,1:T(8,128)(2,1)}), bf16[96,2,128]{2,0,1:T(8,128)(2,1)}) %reduce-scatter.2.cloned.1.call-update) | async-done | bytes 49168 | tf_op jit(solution)/shard_map/reduce_scatter | solution.py:137
  277.2 1.4 convert_element_type.62
  278.6 2.8 fusion.17
  281.4 1.2 fusion.26
  282.6 0.3 fusion.20
  283.0 1.2 fusion.38
  284.2 0.6 copy-done.10
  284.8 1.0 fusion.7
  285.8 0.7 copy.40
  (39 shorter events, 0.2 us)
Async XLA Ops:
  8.0 181.1 %copy-start = (bf16[96,128,128]{2,1,0:T(8,128)(2,1)S(1)}, bf16[96,128,128]{2,1,0:T(8,128)(2,1)}, u32[]{:S(2)}) copy-start(bf16[96,128,128]{2,1,0:T(8,128)(2,1)} %param.13) | copy-start | bytes 9437188
  12.5 7.9 %copy-start.13 = (u32[256]{0:T(256)S(1)}, u32[256]{0:T(256)}, u32[]{:S(2)}) copy-start(u32[256]{0:T(256)} %constant.53) | copy-start | bytes 3076
  12.5 9.1 %copy-start.11 = (s32[24]{0:T(128)S(1)}, s32[24]{0:T(128)}, u32[]{:S(2)}) copy-start(s32[24]{0:T(128)} %param.21) | copy-start | bytes 292
  12.5 9.4 %copy-start.12 = (s32[24,1]{0,1:T(1,128)S(1)}, s32[24,1]{0,1:T(1,128)}, u32[]{:S(2)}) copy-start(s32[24,1]{0,1:T(1,128)} %param.20) | copy-start | bytes 292
  12.5 103.8 %all-to-all-start = ((bf16[32,96,1024]{2,1,0:T(8,128)(2,1)}), bf16[32,96,1024]{2,1,0:T(8,128)(2,1)}, u32[]{:S(2)}, u32[]{:S(2)}) async-start(bf16[32,96,1024]{2,1,0:T(8,128)(2,1)} %stack.2), calls=%async_computation | async-start | bytes 12582912 | tf_op jit(solution)/shard_map/all_to_all | solution.py:113
  20.4 85.3 %copy-start.1 = (bf16[4,2,64,128]{3,2,1,0:T(8,128)(2,1)S(1)}, bf16[4,2,64,128]{3,2,1,0:T(8,128)(2,1)}, u32[]{:S(2)}) copy-start(bf16[4,2,64,128]{3,2,1,0:T(8,128)(2,1)} %param.19) | copy-start | bytes 393220
  20.4 256.8 %reduce-scatter.2.cloned.1.call-start = ((), (), s32[]{:S(2)}) async-start(), calls=%async_computation.3 | async-start | bytes 1622016 | tf_op jit(solution)/shard_map/reduce_scatter | solution.py:137
  185.0 3.4 %copy-start.7 = (bf16[96,1024]{1,0:T(8,128)(2,1)S(1)}, bf16[96,1024]{1,0:T(8,128)(2,1)}, u32[]{:S(2)}) copy-start(bf16[96,1024]{1,0:T(8,128)(2,1)} %param.12) | copy-start | bytes 589828
  185.0 3.5 %copy-start.9 = (s32[96]{0:T(128)S(1)}, s32[96]{0:T(128)}, u32[]{:S(2)}) copy-start(s32[96]{0:T(128)} %param.15) | copy-start | bytes 1156
  187.8 90.8 %all-gather.3.cloned.1.call-start = ((), (), s32[]{:S(2)}) async-start(), calls=%async_computation.2 | async-start | bytes 1769472 | tf_op jit(solution)/shard_map/all_gather | solution.py:103
  188.4 0.7 copy-start.4
  278.6 4.0 %copy-start.5 = (f32[96,8]{1,0:T(8,128)S(1)}, f32[96,8]{1,0:T(8,128)}, u32[]{:S(2)}) copy-start(f32[96,8]{1,0:T(8,128)} %get-tuple-element.9) | copy-start | bytes 9220
  278.6 4.4 %copy-start.2 = (bf16[96,8192]{1,0:T(8,128)(2,1)S(1)}, bf16[96,8192]{1,0:T(8,128)(2,1)}, u32[]{:S(2)}) copy-start(bf16[96,8192]{1,0:T(8,128)(2,1)} %all-gather.3.cloned.1.call-done) | copy-start | bytes 4718596
  278.6 4.4 %copy-start.3 = (bf16[8192,128]{1,0:T(8,128)(2,1)S(1)}, bf16[8192,128]{1,0:T(8,128)(2,1)}, u32[]{:S(2)}) copy-start(bf16[8192,128]{1,0:T(8,128)(2,1)} %param.17) | copy-start | bytes 6291460
  278.6 4.4 %copy-start.6 = (f32[96,2,128]{2,0,1:T(8,128)S(1)}, f32[96,2,128]{2,0,1:T(8,128)}, u32[]{:S(2)}) copy-start(f32[96,2,128]{2,0,1:T(8,128)} %convert_element_type.62) | copy-start | bytes 294916
  281.4 2.8 copy-start.8
  282.9 1.9 copy-start.10
Sparse Core Ops, SparseCore 0:
  187.9 89.2 reduce-scatter.1
Sparse Core Ops, SparseCore 1:
  190.1 43.2 all-gather.2
